TPU v7x, 32 devices: a whole 2x2x4 slice. The times are simulated.
32 devices in a mesh: beam: 1, freq: 32 (over z, y, x, core), tm: 1.
Axes of the slice: x: 2, y: 2, z: 4, core: 2. Of those that a mesh axis runs over, the one named last changes fastest.
Arguments:
- data: bfloat16 [4096, 640], P(('beam', 'freq'), 'tm'), may hold values from -1000 to 1000
- chan_delay: int32 [64, 4096], P(None, 'freq'), may hold values from 0 to 40, as said below
- sub_delay: int32 [2048, 64], P('freq'), may hold values from 0 to 24, as said below
- widths: int32 [16], replicated, may hold values from 1 to 256, as said below
Outputs:
- snr: float32 [2048, 16], P(('beam', 'freq'))
Inputs may be any that keep to these rules, and one draw needn't show every extreme that they name: chan_delay[s, c] is never smaller for a larger trial s; the value 40 is reached. sub_delay[d, b] is never smaller for a larger trial d; the value 24 is reached. The widths are distinct and include 1 and 256.
All inputs are finite; a program needn't handle non-finite values.
Results may differ from a plain program's by a relative error of at most 0.0014.
Values may be sent and summed in bfloat16 or wider, within the bound.
A program may use at most 64 MiB of HBM per device.

v0:
```python
import functools

import jax
import jax.numpy as jnp
from jax import lax
from jax.experimental import pallas as pl
from jax.experimental.pallas import tpu as pltpu
from jax.sharding import PartitionSpec as P

NSUB = 64
NSDM = 64
WMAX = 256
CPS = 64
DPS = 32
D1MAX = 40
D2MAX = 24


def passed_along(value, axis, steps):
    count = lax.axis_size(axis)
    initial, last = (max(0, -steps), min(count, count - steps))
    return lax.ppermute(value, axis, [(source, source + steps) for source in range(initial, last)])


def shifted_sum(source, delays, length, largest):
    band_count = source.shape[0]
    trial_count = delays.shape[1]
    start_total = jnp.zeros((band_count, trial_count, length), jnp.float32)

    def add_shifts(step_index, running_total):
        for within in range(2):
            offset = 2 * step_index + within
            window = lax.dynamic_slice_in_dim(source, offset, length, 2)
            selector = (delays == offset).astype(jnp.bfloat16)
            running_total = running_total + jnp.einsum(
                "bsm,bmt->bst", selector, window, preferred_element_type=jnp.float32
            )
        return running_total

    return lax.fori_loop(0, (largest + 2) // 2, add_shifts, start_total)


def form_subbands(extended, chan_delay, length):
    band_count = extended.shape[0] // CPS
    channel_slabs = extended.reshape(band_count, CPS, extended.shape[1])
    trial_delays = chan_delay.reshape(NSDM, band_count, CPS).transpose(1, 0, 2)
    return shifted_sum(channel_slabs, trial_delays, length, D1MAX).astype(jnp.bfloat16)


def peak_scores(normed, widths, span):
    running = jnp.concatenate(
        [jnp.zeros((normed.shape[0], 1), normed.dtype), jnp.cumsum(normed, axis=1)], axis=1
    )

    def one_width(width):
        upper = lax.dynamic_slice_in_dim(running, width, span, 1)
        return jnp.max((upper - running[:, :span]) / jnp.sqrt(width.astype(jnp.float32)), axis=1)

    return lax.map(one_width, widths).T


def on_device(data, chan_delay, sub_delay, widths):
    block_len = data.shape[1]
    total_len = block_len * lax.axis_size("tm")
    edge_rows = passed_along(data[:, :D1MAX], "tm", -1)
    extended = jnp.concatenate([data, edge_rows], axis=1)
    subband = form_subbands(extended, chan_delay, block_len)
    regrouped = lax.all_to_all(subband, "freq", split_axis=1, concat_axis=0, tiled=True)
    later = passed_along(regrouped[:, :, : D2MAX + WMAX], "tm", -1)
    regrouped = jnp.concatenate([regrouped, later], axis=2)
    dm_len = block_len + WMAX
    local_trials = regrouped.shape[1]
    grouped = sub_delay.reshape(local_trials, DPS, NSUB)
    by_trial = jnp.transpose(regrouped, (1, 0, 2))
    series = shifted_sum(by_trial, grouped, dm_len, D2MAX)
    series = series.reshape(local_trials * DPS, dm_len)
    inside = series[:, :block_len]
    totals = lax.psum(jnp.sum(inside, axis=1), "tm")
    average = totals / total_len
    centred = lax.psum(jnp.sum((inside - average[:, None]) ** 2, axis=1), "tm")
    spread = centred / total_len
    deviation = jnp.sqrt(spread + 1e-05)
    normed = (series - average[:, None]) / deviation[:, None]
    local_peaks = peak_scores(normed, widths, block_len)
    return lax.pmax(local_peaks, "tm")


def fused_kernel(peers, block_len, data_hbm, chan_hbm, sub_hbm, width_hbm, out_ref,
                 data_ref, chan_ref, sub_ref, width_ref, load_sem, times, shifted, select, product, outgoing, incoming,
                 running, send_sem, recv_sem, own_sem):
    me = lax.axis_index("freq")
    rows = data_ref.shape[0]
    bands = rows // CPS
    own_trials = NSDM // peers
    dms = sub_ref.shape[0]
    lanes = 2 * dms
    group = bands * own_trials
    f32, bf16 = jnp.float32, jnp.bfloat16

    barrier = pltpu.get_barrier_semaphore()

    def partner(step):
        return lax.rem(me + step, peers)

    def greet(step, carry):
        pl.semaphore_signal(barrier, inc=1, device_id={"freq": partner(step)},
                            device_id_type=pl.DeviceIdType.MESH)
        return carry

    lax.fori_loop(1, peers, greet, 0)
    loads = [
        pltpu.make_async_copy(source, target, load_sem.at[index])
        for index, (source, target) in enumerate((
            (chan_hbm, chan_ref), (data_hbm, data_ref), (sub_hbm, sub_ref), (width_hbm, width_ref)))
    ]
    for load in loads:
        load.start()

    def iota(shape, axis):
        return lax.broadcasted_iota(jnp.int32, shape, axis)

    def expand(delay_of, largest, width):
        for low in range(8):
            for high in range(largest // 8 + 1):
                if 8 * high + low > largest:
                    block = jnp.zeros((rows, width), bf16)
                else:
                    block = jnp.where(delay_of == float(8 * high + low), 1.0, 0.0).astype(bf16)
                select[low * rows:(low + 1) * rows, high * width:(high + 1) * width] = block

    def products(largest, width):
        highs = largest // 8 + 1
        length = block_len + 8 * highs
        for low in range(8):
            shifted[0:length, low * rows:(low + 1) * rows] = times[low:low + length, :].astype(bf16)
        for start in range(0, length, 352):
            stop = min(start + 352, length)
            product[start:stop, 0:highs * width] = jnp.dot(
                shifted[start:stop, :], select[:, 0:highs * width], preferred_element_type=f32)

    def shifted_total(largest, width):
        highs = largest // 8 + 1
        products(largest, width)
        total = product[0:block_len, 0:width]
        for high in range(1, highs):
            total = total + product[8 * high:8 * high + block_len, high * width:(high + 1) * width]
        return total

    out_cols = NSDM * bands
    spread = (iota((NSDM, out_cols), 1) // bands == iota((NSDM, out_cols), 0)).astype(bf16)
    loads[0].wait()
    chan = chan_ref[...].astype(f32).astype(bf16)
    delay = lax.dot_general(chan, spread, (((0,), (0,)), ((), ())), preferred_element_type=f32)
    same = iota((rows, out_cols), 0) // CPS == iota((rows, out_cols), 1) % bands
    expand(jnp.where(same, delay, -1.0), D1MAX, out_cols)
    loads[1].wait()
    for start in range(0, block_len, 128):
        times[start:start + 128, :] = data_ref[:, start:start + 128].astype(f32).T
    times[block_len:, :] = jnp.zeros((times.shape[0] - block_len, rows), f32)
    subband = shifted_total(D1MAX, out_cols)
    for start in range(0, block_len, 128):
        block = subband[start:start + 128, :].T.astype(bf16)
        outgoing[:, :, start:start + 128] = block.reshape(peers, group, 128)

    pl.semaphore_wait(barrier, peers - 1)

    def sending(step):
        return pltpu.make_async_remote_copy(
            src_ref=outgoing.at[partner(step)], dst_ref=incoming.at[me],
            send_sem=send_sem.at[step], recv_sem=recv_sem.at[step],
            device_id={"freq": partner(step)}, device_id_type=pl.DeviceIdType.MESH)

    def start_one(step, carry):
        sending(step).start()
        return carry

    lax.fori_loop(1, peers, start_one, 0)
    own = pltpu.make_async_copy(outgoing.at[me], incoming.at[me], own_sem)
    own.start()

    trial_dms = dms // own_trials
    band_of = bands * (iota((rows, NSUB), 0) // group) + iota((rows, NSUB), 0) % bands
    pick = (band_of == iota((rows, NSUB), 1)).astype(bf16)
    loads[2].wait()
    loads[3].wait()
    sub = sub_ref[...].astype(f32).astype(bf16)
    delay = lax.dot_general(pick, sub, (((1,), (1,)), ((), ())), preferred_element_type=f32)
    trial_of = (iota((rows, dms), 0) % group) // bands
    same = trial_of == iota((rows, dms), 1) // trial_dms
    expand(jnp.where(same, delay, -1.0), D2MAX, dms)
    below = iota((128, 256), 1) % 128 < iota((128, 256), 0)
    below = below.astype(f32).astype(bf16)

    def finish_one(step, carry):
        sending(step).wait()
        return carry

    own.wait()
    lax.fori_loop(1, peers, finish_one, 0)

    for start in range(0, block_len, 128):
        block = incoming[:, :, start:start + 128].reshape(rows, 128)
        times[start:start + 128, :] = block.astype(f32).T
    products(D2MAX, dms)
    pairs = (D2MAX // 8 + 1) // 2
    mixed = product[0:block_len + 8, 0:lanes]
    for pair in range(1, pairs):
        mixed = mixed + product[16 * pair:16 * pair + block_len + 8, pair * lanes:(pair + 1) * lanes]
    swapped = pltpu.roll(mixed, dms, 1)
    on_left = iota((block_len, lanes), 1) < dms
    series = (jnp.where(on_left, mixed[0:block_len], swapped[0:block_len])
              + jnp.where(on_left, swapped[8:], mixed[8:]))
    average = jnp.sum(series, axis=0, keepdims=True) / block_len
    centred = series - average
    spread = jnp.sum(centred * centred, axis=0, keepdims=True) / block_len
    deviation = jnp.sqrt(spread + 1e-05)
    carry = jnp.zeros((1, lanes), f32)
    for start in range(0, block_len, 128):
        block = centred[start:start + 128, :]
        head = block.astype(bf16)
        tail = (block - head.astype(f32)).astype(bf16)
        sums = jnp.dot(below, jnp.concatenate([head, tail], axis=0), preferred_element_type=f32) + carry
        running[start:start + 128, :] = sums
        carry = sums[127:128, :] + block[127:128, :]
    after = iota((WMAX, lanes), 0).astype(f32)
    running[block_len:block_len + WMAX, :] = carry - average * after

    half = block_len // 2
    left = iota((half + WMAX, lanes), 1) < dms
    running[0:half + WMAX, :] = jnp.where(left, running[0:half + WMAX, :], running[half:block_len + WMAX, :])
    base = running[0:half, :]
    peaks = []
    for index in range(width_ref.shape[0]):
        width = width_ref[index]
        upper = running[pl.ds(width, half), :]
        peak = jnp.max(upper - base, axis=0, keepdims=True)
        scale = jnp.sqrt(jnp.full((1, lanes), width.astype(f32)))
        peaks.append(peak / (deviation * scale))
    peaks = jnp.concatenate(peaks, axis=0)
    peaks = jnp.maximum(peaks, pltpu.roll(peaks, dms, 1))
    out_ref[...] = peaks[:, 0:dms]


def fused(data, chan_delay, sub_delay, widths):
    peers = lax.axis_size("freq")
    rows, block_len = data.shape
    bands = rows // CPS
    dms = sub_delay.shape[0]
    group = bands * (NSDM // peers)
    length = block_len + D1MAX + 8
    wide = (D1MAX // 8 + 1) * NSDM * bands
    anywhere = pl.BlockSpec(memory_space=pl.ANY)
    peaks = pl.pallas_call(
        functools.partial(fused_kernel, peers, block_len),
        out_shape=pltpu.VMEM((widths.shape[0], dms), jnp.float32),
        in_specs=[anywhere] * 4,
        out_specs=pl.BlockSpec(memory_space=pltpu.VMEM),
        scratch_shapes=[
            pltpu.VMEM(data.shape, data.dtype),
            pltpu.VMEM(chan_delay.shape, chan_delay.dtype),
            pltpu.VMEM(sub_delay.shape, sub_delay.dtype),
            pltpu.SMEM(widths.shape, widths.dtype),
            pltpu.SemaphoreType.DMA((4,)),
            pltpu.VMEM((length + 8, rows), jnp.float32),
            pltpu.VMEM((length, 8 * rows), jnp.bfloat16),
            pltpu.VMEM((8 * rows, wide), jnp.bfloat16),
            pltpu.VMEM((length, wide), jnp.float32),
            pltpu.VMEM((peers, group, block_len), jnp.bfloat16),
            pltpu.VMEM((peers, group, block_len), jnp.bfloat16),
            pltpu.VMEM((block_len + WMAX, 2 * dms), jnp.float32),
            pltpu.SemaphoreType.DMA((peers,)),
            pltpu.SemaphoreType.DMA((peers,)),
            pltpu.SemaphoreType.DMA,
        ],
        compiler_params=pltpu.CompilerParams(collective_id=0, has_side_effects=True),
    )(data, chan_delay, sub_delay, widths)
    return peaks.T


def solution(mesh):
    in_specs = (P(("beam", "freq"), "tm"), P(None, "freq"), P("freq", None), P())
    out_specs = P(("beam", "freq"), None)
    whole_time = mesh.shape["tm"] == 1
    return jax.shard_map(
        fused if whole_time else on_device, mesh=mesh, in_specs=in_specs, out_specs=out_specs, check_vma=False
    )
```

profile of v0, /device:TPU:0, one launch (start us, length us, event | category | flops | bytes accessed | tf_op | source)
XLA Modules:
  0.0 14.5 jit_solution(17566271945896490348)
XLA Ops:
  0.0 13.9 %shard_map.46 = f32[16,64]{1,0:T(8,128)S(1)} custom-call(bf16[128,640]{1,0:T(8,128)(2,1)} %data_hbm.1, s32[64,128]{1,0:T(8,128)} %chan_hbm.1, s32[64,64]{1,0:T(8,128)} %sub_hbm.1, s32[16]{0:T(128)} %width_hbm.1), custom_call_target="tpu_custom_call" | custom-call | tf_op jit(solution)/shard_map/pallas_call | solution.py:253
  13.9 0.6 %copy.6 = f32[64,16]{0,1:T(8,128)} copy(f32[64,16]{0,1:T(8,128)S(1)} %bitcast.1) | data formatting | bytes 8192
where the time goes:
time: 14.6 us; the launch traced here: 14.5 us
  Pallas kernels  13.9 us (95%)
  local copies, waits for them, and re-layouts  0.6 us (4%)
    pallas_call x1, Pallas kernels, fused(): pl.pallas_call(functools.partial(fused_kernel, peers, block_len), out_sha...  13.9 us
    unnamed x1, local copies, waits for them, and re-layouts  0.6 us

commit v1 on v0

v1 whole, which is shorter than its diff:
```python
import functools

import jax
import jax.numpy as jnp
from jax import lax
from jax.experimental import pallas as pl
from jax.experimental.pallas import tpu as pltpu
from jax.sharding import PartitionSpec as P

NSUB = 64
NSDM = 64
WMAX = 256
CPS = 64
DPS = 32
D1MAX = 40
D2MAX = 24


def passed_along(value, axis, steps):
    count = lax.axis_size(axis)
    initial, last = (max(0, -steps), min(count, count - steps))
    return lax.ppermute(value, axis, [(source, source + steps) for source in range(initial, last)])


def shifted_sum(source, delays, length, largest):
    band_count = source.shape[0]
    trial_count = delays.shape[1]
    start_total = jnp.zeros((band_count, trial_count, length), jnp.float32)

    def add_shifts(step_index, running_total):
        for within in range(2):
            offset = 2 * step_index + within
            window = lax.dynamic_slice_in_dim(source, offset, length, 2)
            selector = (delays == offset).astype(jnp.bfloat16)
            running_total = running_total + jnp.einsum(
                "bsm,bmt->bst", selector, window, preferred_element_type=jnp.float32
            )
        return running_total

    return lax.fori_loop(0, (largest + 2) // 2, add_shifts, start_total)


def form_subbands(extended, chan_delay, length):
    band_count = extended.shape[0] // CPS
    channel_slabs = extended.reshape(band_count, CPS, extended.shape[1])
    trial_delays = chan_delay.reshape(NSDM, band_count, CPS).transpose(1, 0, 2)
    return shifted_sum(channel_slabs, trial_delays, length, D1MAX).astype(jnp.bfloat16)


def prefix_sums(values):
    step = 1
    while step < values.shape[1]:
        values = values + jnp.pad(values[:, :-step], ((0, 0), (step, 0)))
        step *= 2
    return values


def peak_scores(normed, widths, span):
    running = jnp.concatenate([jnp.zeros((normed.shape[0], 1), normed.dtype), prefix_sums(normed)], axis=1)

    def one_width(width):
        upper = lax.dynamic_slice_in_dim(running, width, span, 1)
        return jnp.max((upper - running[:, :span]) / jnp.sqrt(width.astype(jnp.float32)), axis=1)

    return lax.map(one_width, widths).T


def on_device(data, chan_delay, sub_delay, widths):
    block_len = data.shape[1]
    total_len = block_len * lax.axis_size("tm")
    edge_rows = passed_along(data[:, :D1MAX], "tm", -1)
    extended = jnp.concatenate([data, edge_rows], axis=1)
    subband = form_subbands(extended, chan_delay, block_len)
    regrouped = lax.all_to_all(subband, "freq", split_axis=1, concat_axis=0, tiled=True)
    later = passed_along(regrouped[:, :, : D2MAX + WMAX], "tm", -1)
    regrouped = jnp.concatenate([regrouped, later], axis=2)
    dm_len = block_len + WMAX
    local_trials = regrouped.shape[1]
    grouped = sub_delay.reshape(local_trials, DPS, NSUB)
    by_trial = jnp.transpose(regrouped, (1, 0, 2))
    series = shifted_sum(by_trial, grouped, dm_len, D2MAX)
    series = series.reshape(local_trials * DPS, dm_len)
    inside = series[:, :block_len]
    totals = lax.psum(jnp.sum(inside, axis=1), "tm")
    average = totals / total_len
    centred = lax.psum(jnp.sum((inside - average[:, None]) ** 2, axis=1), "tm")
    spread = centred / total_len
    deviation = jnp.sqrt(spread + 1e-05)
    normed = (series - average[:, None]) / deviation[:, None]
    local_peaks = peak_scores(normed, widths, block_len)
    return lax.pmax(local_peaks, "tm")

LOWS = 4


def fused_kernel(peers, block_len, data_hbm, chan_hbm, sub_hbm, width_hbm, out_ref,
                 data_ref, chan_ref, sub_ref, width_ref, load_sem, select, shifted, picks, moved, outgoing, incoming,
                 running, send_sem, recv_sem):
    me = lax.axis_index("freq")
    rows = data_ref.shape[0]
    bands = rows // CPS
    own_trials = NSDM // peers
    dms = sub_ref.shape[0]
    group = bands * own_trials
    f32, bf16 = jnp.float32, jnp.bfloat16
    highs = D1MAX // LOWS + 1
    sub_highs = D2MAX // LOWS + 1
    blocks = block_len // 128

    loads = [
        pltpu.make_async_copy(source, target, load_sem.at[index])
        for index, (source, target) in enumerate((
            (chan_hbm, chan_ref), (data_hbm, data_ref), (sub_hbm, sub_ref), (width_hbm, width_ref)))
    ]
    for load in loads:
        load.start()

    barrier = pltpu.get_barrier_semaphore()

    def greet(step, carry):
        pl.semaphore_signal(barrier, inc=1, device_id={"freq": lax.rem(me + step, peers)},
                            device_id_type=pl.DeviceIdType.MESH)
        return carry

    lax.fori_loop(1, peers, greet, 0)

    def iota(shape, axis):
        return lax.broadcasted_iota(jnp.int32, shape, axis)

    def shift_rows(block, target, first, count):
        wide = block.astype(f32)
        lane = iota(wide.shape, 1)
        for low in range(LOWS):
            piece = wide
            if low:
                piece = jnp.where(lane < block_len - low, pltpu.roll(wide, block_len - low, 1), 0.0)
            target[low * count + first:low * count + first + wide.shape[0], :] = piece.astype(bf16)

    def total_of(product, count, count_highs):
        lane = iota((count, 128), 1)
        sums = [product[0:count, 128 * i:128 * (i + 1)] for i in range(blocks)]
        for high in range(1, count_highs):
            step = LOWS * high
            turned = [
                pltpu.roll(product[high * count:(high + 1) * count, 128 * i:128 * (i + 1)], 128 - step, 1)
                for i in range(blocks)
            ] + [0.0]
            for i in range(blocks):
                sums[i] = sums[i] + jnp.where(lane < 128 - step, turned[i], turned[i + 1])
        return sums

    def pick_trials(first, count):
        lane = iota((count, rows), 1)
        chan = chan_ref[first:first + count, :]
        other = pltpu.roll(chan, CPS, 1)
        for band in range(bands):
            near, far = (chan, other) if band == 0 else (other, chan)
            pair = jnp.where(lane < CPS, near, far - 1)
            for high in range(highs):
                for half in range(LOWS // 2):
                    block = jnp.where(pair == LOWS * high + 2 * half, 1.0, 0.0).astype(bf16)
                    start = highs * first + high * count
                    select[band, start:start + count, 128 * half:128 * (half + 1)] = block

    def form(first, count):
        for band in range(bands):
            start = highs * first
            product = jnp.dot(select[band, start:start + highs * count, :], shifted[band],
                              preferred_element_type=f32)
            sums = total_of(product, count, highs)
            for i in range(blocks):
                outgoing[first // own_trials:(first + count) // own_trials, own_trials * band:own_trials * (band + 1),
                         128 * i:128 * (i + 1)] = sums[i].astype(bf16).reshape(count // own_trials, own_trials, 128)

    quarter = peers // 4

    def sending(target):
        return pltpu.make_async_remote_copy(
            src_ref=outgoing.at[target], dst_ref=incoming.at[me],
            send_sem=send_sem, recv_sem=recv_sem.at[me // quarter],
            device_id={"freq": target}, device_id_type=pl.DeviceIdType.MESH)

    def start_one(target, carry):
        @pl.when(target != me)
        def _():
            sending(target).start()
        return carry

    first_trials = NSDM // 4
    loads[0].wait()
    pick_trials(0, first_trials)
    loads[1].wait()
    for band in range(bands):
        shift_rows(data_ref[band * CPS:(band + 1) * CPS, :], shifted.at[band], 0, CPS)
    form(0, first_trials)
    pl.semaphore_wait(barrier, peers - 1)
    lax.fori_loop(0, quarter, start_one, 0)
    pick_trials(first_trials, NSDM - first_trials)
    form(first_trials, NSDM - first_trials)
    lax.fori_loop(quarter, peers, start_one, 0)
    own = pltpu.make_async_copy(outgoing.at[me], incoming.at[me], recv_sem.at[me // quarter])
    own.start()

    loads[2].wait()
    loads[3].wait()
    trial_dms = dms // own_trials
    half_rows = rows // 2
    sub = sub_ref[...].astype(f32).astype(bf16)
    for half in range(2):
        lane = iota((NSUB, 128), 1)
        row = half * half_rows + lane % half_rows
        spread = (row // own_trials == iota((NSUB, 128), 0)).astype(f32).astype(bf16)
        delay = jnp.dot(sub, spread, preferred_element_type=f32)
        lane = iota((dms, 128), 1)
        delay = delay - (lane // half_rows).astype(f32)
        delay = jnp.where(lane % own_trials == iota((dms, 128), 0) // trial_dms, delay, -99.0)
        for high in range(sub_highs):
            for pair in range(LOWS // 2):
                picks[half, high * dms:(high + 1) * dms, 128 * pair:128 * (pair + 1)] = jnp.where(
                    delay == float(LOWS * high + 2 * pair), 1.0, 0.0).astype(bf16)
    below = (iota((136, 256), 1) % 128 < iota((136, 256), 0)).astype(f32).astype(bf16)

    def arrived(index):
        part = incoming.at[index * quarter:(index + 1) * quarter]
        pltpu.make_async_copy(part, part, recv_sem.at[index]).wait()
        block = jnp.concatenate(
            [incoming[index * quarter:(index + 1) * quarter, :, 128 * i:128 * (i + 1)].reshape(rows // 4, 128)
             for i in range(blocks)], axis=1)
        shift_rows(block, moved.at[index // 2], index % 2 * (rows // 4), half_rows)

    def half_series(half):
        product = jnp.dot(picks[half], moved[half], preferred_element_type=f32)
        return total_of(product, dms, sub_highs)

    arrived(0)
    arrived(1)
    early = half_series(0)
    arrived(2)
    arrived(3)
    late = half_series(1)
    sent = outgoing.at[0:peers - 1]
    pltpu.make_async_copy(sent, sent, send_sem).wait()

    series = [a + b for a, b in zip(early, late)]
    average = jnp.sum(sum(series), axis=1, keepdims=True) / block_len
    centred = [block - average for block in series]
    spread = jnp.sum(sum(block * block for block in centred), axis=1, keepdims=True) / block_len
    deviation = jnp.sqrt(spread + 1e-05)
    across = jnp.broadcast_to(deviation, (dms, 128)).T[0:1, :]
    centred = centred + [jnp.broadcast_to(-average, (dms, 128))] * (WMAX // 128)
    heads = [block.astype(bf16) for block in centred]
    tails = [(block - head.astype(f32)).astype(bf16) for block, head in zip(centred, heads)]
    ahead = blocks + WMAX // 128 - blocks
    carry = jnp.zeros((1, 2 * dms), f32)
    for i in range(blocks):
        j = i + 2
        block = jnp.concatenate([
            jnp.concatenate([heads[i], tails[i]], axis=1), jnp.concatenate([heads[j], tails[j]], axis=1)], axis=0)
        sums = lax.dot_general(below, block, (((1,), (1,)), ((), ())), preferred_element_type=f32)
        running[128 * i:128 * (i + 1), :] = sums[0:128, :] + carry
        carry = carry + sums[128:129, :]

    span = block_len - 256
    base = running[0:span, :]
    peaks = []
    for index in range(width_ref.shape[0]):
        width = width_ref[index]
        upper = running[pl.ds(width, span), :]
        peaks.append(jnp.max(upper - base, axis=0, keepdims=True))
    peaks = jnp.concatenate(peaks, axis=0)
    peaks = jnp.maximum(peaks, pltpu.roll(peaks, dms, 1))
    scales = jnp.concatenate(
        [jnp.full((1, dms), width_ref[index].astype(f32)) for index in range(width_ref.shape[0])], axis=0)
    out_ref[...] = peaks[:, 0:dms] / (across * jnp.sqrt(scales))


def fused(data, chan_delay, sub_delay, widths):
    peers = lax.axis_size("freq")
    rows, block_len = data.shape
    bands = rows // CPS
    dms = sub_delay.shape[0]
    group = bands * (NSDM // peers)
    highs = D1MAX // LOWS + 1
    sub_highs = D2MAX // LOWS + 1
    anywhere = pl.BlockSpec(memory_space=pl.ANY)
    peaks = pl.pallas_call(
        functools.partial(fused_kernel, peers, block_len),
        out_shape=pltpu.VMEM((widths.shape[0], dms), jnp.float32),
        in_specs=[anywhere] * 4,
        out_specs=pl.BlockSpec(memory_space=pltpu.VMEM),
        scratch_shapes=[
            pltpu.VMEM(data.shape, data.dtype),
            pltpu.VMEM(chan_delay.shape, chan_delay.dtype),
            pltpu.VMEM(sub_delay.shape, sub_delay.dtype),
            pltpu.SMEM(widths.shape, widths.dtype),
            pltpu.SemaphoreType.DMA((4,)),
            pltpu.VMEM((bands, highs * NSDM, LOWS * CPS), jnp.bfloat16),
            pltpu.VMEM((bands, LOWS * CPS, block_len), jnp.bfloat16),
            pltpu.VMEM((2, sub_highs * dms, LOWS * rows // 2), jnp.bfloat16),
            pltpu.VMEM((2, LOWS * rows // 2, block_len), jnp.bfloat16),
            pltpu.VMEM((peers, group, block_len), jnp.bfloat16),
            pltpu.VMEM((peers, group, block_len), jnp.bfloat16),
            pltpu.VMEM((block_len, 2 * dms), jnp.float32),
            pltpu.SemaphoreType.DMA,
            pltpu.SemaphoreType.DMA((4,)),
        ],
        compiler_params=pltpu.CompilerParams(collective_id=0, has_side_effects=True),
    )(data, chan_delay, sub_delay, widths)
    return peaks.T


def solution(mesh):
    in_specs = (P(("beam", "freq"), "tm"), P(None, "freq"), P("freq", None), P())
    out_specs = P(("beam", "freq"), None)
    whole_time = mesh.shape["tm"] == 1
    return jax.shard_map(
        fused if whole_time else on_device, mesh=mesh, in_specs=in_specs, out_specs=out_specs, check_vma=False
    )
```

time: 14.6 us -> 13.6 us (0.932)
  the two profiles are of different devices: /device:TPU:0 before, /device:TPU:31 now
where the time goes in v1:
time: 13.6 us; the launch traced here: 13.5 us
  Pallas kernels  12.9 us (95%)
  local copies, waits for them, and re-layouts  0.6 us (4%)
    pallas_call x1, Pallas kernels, fused(): pl.pallas_call(functools.partial(fused_kernel, peers, block_len), out_sha...  12.9 us
    unnamed x1, local copies, waits for them, and re-layouts  0.6 us

profile of v1, /device:TPU:31, one launch (start us, length us, event | category | flops | bytes accessed | tf_op | source)
XLA Modules:
  0.0 13.5 jit_solution(6832651599596366971)
XLA Ops:
  0.0 12.9 %shard_map.46 = f32[16,64]{1,0:T(8,128)S(1)} custom-call(bf16[128,640]{1,0:T(8,128)(2,1)} %data_hbm.1, s32[64,128]{1,0:T(8,128)} %chan_hbm.1, s32[64,64]{1,0:T(8,128)} %sub_hbm.1, s32[16]{0:T(128)} %width_hbm.1), custom_call_target="tpu_custom_call" | custom-call | tf_op jit(solution)/shard_map/pallas_call | solution.py:286
  12.9 0.6 %copy.6 = f32[64,16]{0,1:T(8,128)} copy(f32[64,16]{0,1:T(8,128)S(1)} %bitcast.1) | data formatting | bytes 8192

commit v2 on v1

--- a/solution.py
+++ b/solution.py
@@ -193,11 +193,10 @@
     for band in range(bands):
         shift_rows(data_ref[band * CPS:(band + 1) * CPS, :], shifted.at[band], 0, CPS)
     form(0, first_trials)
-    pl.semaphore_wait(barrier, peers - 1)
-    lax.fori_loop(0, quarter, start_one, 0)
     pick_trials(first_trials, NSDM - first_trials)
     form(first_trials, NSDM - first_trials)
-    lax.fori_loop(quarter, peers, start_one, 0)
+    pl.semaphore_wait(barrier, peers - 1)
+    lax.fori_loop(0, peers, start_one, 0)
     own = pltpu.make_async_copy(outgoing.at[me], incoming.at[me], recv_sem.at[me // quarter])
     own.start()
 
@@ -238,8 +237,6 @@
     arrived(2)
     arrived(3)
     late = half_series(1)
-    sent = outgoing.at[0:peers - 1]
-    pltpu.make_async_copy(sent, sent, send_sem).wait()
 
     series = [a + b for a, b in zip(early, late)]
     average = jnp.sum(sum(series), axis=1, keepdims=True) / block_len
@@ -272,6 +269,8 @@
     scales = jnp.concatenate(
         [jnp.full((1, dms), width_ref[index].astype(f32)) for index in range(width_ref.shape[0])], axis=0)
     out_ref[...] = peaks[:, 0:dms] / (across * jnp.sqrt(scales))
+    sent = outgoing.at[0:peers - 1]
+    pltpu.make_async_copy(sent, sent, send_sem).wait()
 
 
 def fused(data, chan_delay, sub_delay, widths):

time: 13.6 us -> 13.2 us (0.971)
  the two profiles are of different devices: /device:TPU:31 before, /device:TPU:0 now
where the time goes in v2:
time: 13.2 us; the launch traced here: 13 us
  Pallas kernels  12.4 us (94%)
  local copies, waits for them, and re-layouts  0.6 us (5%)
    pallas_call x1, Pallas kernels, fused(): pl.pallas_call(functools.partial(fused_kernel, peers, block_len), out_sha...  12.4 us
    unnamed x1, local copies, waits for them, and re-layouts  0.6 us

profile of v2, /device:TPU:0, one launch (start us, length us, event | category | flops | bytes accessed | tf_op | source)
XLA Modules:
  0.0 13.0 jit_solution(1936853337562852313)
XLA Ops:
  0.0 12.4 %shard_map.46 = f32[16,64]{1,0:T(8,128)S(1)} custom-call(bf16[128,640]{1,0:T(8,128)(2,1)} %data_hbm.1, s32[64,128]{1,0:T(8,128)} %chan_hbm.1, s32[64,64]{1,0:T(8,128)} %sub_hbm.1, s32[16]{0:T(128)} %width_hbm.1), custom_call_target="tpu_custom_call" | custom-call | tf_op jit(solution)/shard_map/pallas_call | solution.py:285
  12.4 0.6 %copy.6 = f32[64,16]{0,1:T(8,128)} copy(f32[64,16]{0,1:T(8,128)S(1)} %bitcast.1) | data formatting | bytes 8192

commit v3 on v2

--- a/solution.py
+++ b/solution.py
@@ -95,7 +95,7 @@
 
 def fused_kernel(peers, block_len, data_hbm, chan_hbm, sub_hbm, width_hbm, out_ref,
                  data_ref, chan_ref, sub_ref, width_ref, load_sem, select, shifted, picks, moved, outgoing, incoming,
-                 running, send_sem, recv_sem):
+                 running, totals, send_sem, recv_sem):
     me = lax.axis_index("freq")
     rows = data_ref.shape[0]
     bands = rows // CPS
@@ -128,13 +128,12 @@
         return lax.broadcasted_iota(jnp.int32, shape, axis)
 
     def shift_rows(block, target, first, count):
-        wide = block.astype(f32)
-        lane = iota(wide.shape, 1)
+        lane = iota(block.shape, 1)
         for low in range(LOWS):
-            piece = wide
+            piece = block
             if low:
-                piece = jnp.where(lane < block_len - low, pltpu.roll(wide, block_len - low, 1), 0.0)
-            target[low * count + first:low * count + first + wide.shape[0], :] = piece.astype(bf16)
+                piece = jnp.where(lane < block_len - low, pltpu.roll(block, block_len - low, 1), jnp.zeros_like(block))
+            target[low * count + first:low * count + first + block.shape[0], :] = piece
 
     def total_of(product, count, count_highs):
         lane = iota((count, 128), 1)
@@ -217,53 +216,56 @@
             for pair in range(LOWS // 2):
                 picks[half, high * dms:(high + 1) * dms, 128 * pair:128 * (pair + 1)] = jnp.where(
                     delay == float(LOWS * high + 2 * pair), 1.0, 0.0).astype(bf16)
-    below = (iota((136, 256), 1) % 128 < iota((136, 256), 0)).astype(f32).astype(bf16)
-
-    def arrived(index):
-        part = incoming.at[index * quarter:(index + 1) * quarter]
+    before = jnp.where(iota((256, 256), 1) < 128, iota((256, 256), 0) % 128 - iota((256, 256), 1), -1) < 0
+    totals[...] = before.astype(f32).astype(bf16)
+
+    def arrived(index, place):
+        part = incoming.at[pl.ds(index * quarter, quarter)]
         pltpu.make_async_copy(part, part, recv_sem.at[index]).wait()
         block = jnp.concatenate(
-            [incoming[index * quarter:(index + 1) * quarter, :, 128 * i:128 * (i + 1)].reshape(rows // 4, 128)
+            [incoming[pl.ds(index * quarter, quarter), :, 128 * i:128 * (i + 1)].reshape(rows // 4, 128)
              for i in range(blocks)], axis=1)
-        shift_rows(block, moved.at[index // 2], index % 2 * (rows // 4), half_rows)
+        shift_rows(block, moved.at[index // 2], place * (rows // 4), half_rows)
 
     def half_series(half):
-        product = jnp.dot(picks[half], moved[half], preferred_element_type=f32)
-        return total_of(product, dms, sub_highs)
-
-    arrived(0)
-    arrived(1)
-    early = half_series(0)
-    arrived(2)
-    arrived(3)
-    late = half_series(1)
-
-    series = [a + b for a, b in zip(early, late)]
+        arrived(2 * half, 0)
+        arrived(2 * half + 1, 1)
+        return total_of(jnp.dot(picks[half], moved[half], preferred_element_type=f32), dms, sub_highs)
+
+    near = (2 * me) // peers
+    series = [a + b for a, b in zip(half_series(near), half_series(1 - near))]
     average = jnp.sum(sum(series), axis=1, keepdims=True) / block_len
     centred = [block - average for block in series]
     spread = jnp.sum(sum(block * block for block in centred), axis=1, keepdims=True) / block_len
     deviation = jnp.sqrt(spread + 1e-05)
     across = jnp.broadcast_to(deviation, (dms, 128)).T[0:1, :]
-    centred = centred + [jnp.broadcast_to(-average, (dms, 128))] * (WMAX // 128)
-    heads = [block.astype(bf16) for block in centred]
-    tails = [(block - head.astype(f32)).astype(bf16) for block, head in zip(centred, heads)]
-    ahead = blocks + WMAX // 128 - blocks
-    carry = jnp.zeros((1, 2 * dms), f32)
+    stacked = jnp.concatenate(centred, axis=0)
+    head = stacked.astype(bf16)
+    tail = (stacked - head.astype(f32)).astype(bf16)
+    sums = jnp.dot(jnp.concatenate([head, tail], axis=1), totals[...], preferred_element_type=f32)
+    carry = jnp.zeros((dms, 128), f32)
+    pieces = []
     for i in range(blocks):
-        j = i + 2
-        block = jnp.concatenate([
-            jnp.concatenate([heads[i], tails[i]], axis=1), jnp.concatenate([heads[j], tails[j]], axis=1)], axis=0)
-        sums = lax.dot_general(below, block, (((1,), (1,)), ((), ())), preferred_element_type=f32)
-        running[128 * i:128 * (i + 1), :] = sums[0:128, :] + carry
-        carry = carry + sums[128:129, :]
+        block = sums[i * dms:(i + 1) * dms, :]
+        pieces.append(block[:, 0:128] + carry)
+        carry = carry + block[:, 128:256]
+    for i in range(WMAX // 128):
+        pieces.append(carry - average * (iota((dms, 128), 1) + 128 * i).astype(f32))
+    for i in range(blocks):
+        running[128 * i:128 * (i + 1), :] = jnp.concatenate([pieces[i], pieces[i + 2]], axis=0).T
 
     span = block_len - 256
-    base = running[0:span, :]
-    peaks = []
-    for index in range(width_ref.shape[0]):
-        width = width_ref[index]
-        upper = running[pl.ds(width, span), :]
-        peaks.append(jnp.max(upper - base, axis=0, keepdims=True))
+    tile = 64
+    count = width_ref.shape[0]
+    widths = [width_ref[index] for index in range(count)]
+    best = [None] * count
+    for start in range(0, span, tile):
+        base = running[start:start + tile, :]
+        for index in range(count):
+            rise = running[pl.ds(widths[index] + start, tile), :] - base
+            rise = jnp.max(rise.reshape(tile // 8, 8, 2 * dms), axis=0)
+            best[index] = rise if start == 0 else jnp.maximum(best[index], rise)
+    peaks = [jnp.max(rise, axis=0, keepdims=True) for rise in best]
     peaks = jnp.concatenate(peaks, axis=0)
     peaks = jnp.maximum(peaks, pltpu.roll(peaks, dms, 1))
     scales = jnp.concatenate(
@@ -300,6 +302,7 @@
             pltpu.VMEM((peers, group, block_len), jnp.bfloat16),
             pltpu.VMEM((peers, group, block_len), jnp.bfloat16),
             pltpu.VMEM((block_len, 2 * dms), jnp.float32),
+            pltpu.VMEM((256, 256), jnp.bfloat16),
             pltpu.SemaphoreType.DMA,
             pltpu.SemaphoreType.DMA((4,)),
         ],

time: 13.2 us -> 13 us (0.985)
    pallas_call x1, Pallas kernels: 12.4 us -> 12.3 us  [fused(): pl.pallas_call(functools.partial(fused_kernel, peers, block_len), out_sha...]
where the time goes in v3:
time: 13 us; the launch traced here: 12.9 us
  Pallas kernels  12.3 us (95%)
  local copies, waits for them, and re-layouts  0.6 us (5%)
    pallas_call x1, Pallas kernels, fused(): pl.pallas_call(functools.partial(fused_kernel, peers, block_len), out_sha...  12.3 us
    unnamed x1, local copies, waits for them, and re-layouts  0.6 us

profile of v3, /device:TPU:0, one launch (start us, length us, event | category | flops | bytes accessed | tf_op | source)
XLA Modules:
  0.0 12.9 jit_solution(5534238576788687652)
XLA Ops:
  0.0 12.3 %shard_map.46 = f32[16,64]{1,0:T(8,128)S(1)} custom-call(bf16[128,640]{1,0:T(8,128)(2,1)} %data_hbm.1, s32[64,128]{1,0:T(8,128)} %chan_hbm.1, s32[64,64]{1,0:T(8,128)} %sub_hbm.1, s32[16]{0:T(128)} %width_hbm.1), custom_call_target="tpu_custom_call" | custom-call | tf_op jit(solution)/shard_map/pallas_call | solution.py:287
  12.3 0.6 %copy.6 = f32[64,16]{0,1:T(8,128)} copy(f32[64,16]{0,1:T(8,128)S(1)} %bitcast.1) | data formatting | bytes 8192

commit v4 on v3

--- a/solution.py
+++ b/solution.py
@@ -192,10 +192,25 @@
     for band in range(bands):
         shift_rows(data_ref[band * CPS:(band + 1) * CPS, :], shifted.at[band], 0, CPS)
     form(0, first_trials)
+    last = me >= peers - 2
+
+    def meet():
+        pl.semaphore_wait(barrier, peers - 1)
+        lax.fori_loop(0, 2, start_one, 0)
+
+    pl.when(last)(meet)
     pick_trials(first_trials, NSDM - first_trials)
     form(first_trials, NSDM - first_trials)
-    pl.semaphore_wait(barrier, peers - 1)
-    lax.fori_loop(0, peers, start_one, 0)
+    pl.when(jnp.logical_not(last))(meet)
+
+    def start_rest(step, carry):
+        target = lax.rem(me + step, peers)
+        @pl.when(target >= 2)
+        def _():
+            start_one(target, carry)
+        return carry
+
+    lax.fori_loop(0, peers, start_rest, 0)
     own = pltpu.make_async_copy(outgoing.at[me], incoming.at[me], recv_sem.at[me // quarter])
     own.start()
 
@@ -314,7 +329,7 @@
 def solution(mesh):
     in_specs = (P(("beam", "freq"), "tm"), P(None, "freq"), P("freq", None), P())
     out_specs = P(("beam", "freq"), None)
-    whole_time = mesh.shape["tm"] == 1
+    whole_time = mesh.shape["tm"] == 1 and mesh.shape["freq"] % 8 == 0
     return jax.shard_map(
         fused if whole_time else on_device, mesh=mesh, in_specs=in_specs, out_specs=out_specs, check_vma=False
     )

time: 13 us -> 12.8 us (0.985)
  Pallas kernels: 12.3 us -> 12 us
    pallas_call x1, Pallas kernels: 12.3 us -> 12 us  [fused(): pl.pallas_call(functools.partial(fused_kernel, peers, block_len), out_sha...]
where the time goes in v4:
time: 12.8 us; the launch traced here: 12.6 us
  Pallas kernels  12 us (94%)
  local copies, waits for them, and re-layouts  0.6 us (5%)
    pallas_call x1, Pallas kernels, fused(): pl.pallas_call(functools.partial(fused_kernel, peers, block_len), out_sha...  12 us
    unnamed x1, local copies, waits for them, and re-layouts  0.6 us

profile of v4, /device:TPU:0, one launch (start us, length us, event | category | flops | bytes accessed | tf_op | source)
XLA Modules:
  0.0 12.6 jit_solution(1055323855598504277)
XLA Ops:
  0.0 12.0 %shard_map.46 = f32[16,64]{1,0:T(8,128)S(1)} custom-call(bf16[128,640]{1,0:T(8,128)(2,1)} %data_hbm.1, s32[64,128]{1,0:T(8,128)} %chan_hbm.1, s32[64,64]{1,0:T(8,128)} %sub_hbm.1, s32[16]{0:T(128)} %width_hbm.1), custom_call_target="tpu_custom_call" | custom-call | tf_op jit(solution)/shard_map/pallas_call | solution.py:302
  12.0 0.6 %copy.6 = f32[64,16]{0,1:T(8,128)} copy(f32[64,16]{0,1:T(8,128)S(1)} %bitcast.1) | data formatting | bytes 8192

commit v5 on v4

--- a/solution.py
+++ b/solution.py
@@ -91,6 +91,7 @@
     return lax.pmax(local_peaks, "tm")
 
 LOWS = 4
+SUB_LOWS = 8
 
 
 def fused_kernel(peers, block_len, data_hbm, chan_hbm, sub_hbm, width_hbm, out_ref,
@@ -104,7 +105,7 @@
     group = bands * own_trials
     f32, bf16 = jnp.float32, jnp.bfloat16
     highs = D1MAX // LOWS + 1
-    sub_highs = D2MAX // LOWS + 1
+    sub_highs = D2MAX // SUB_LOWS + 1
     blocks = block_len // 128
 
     loads = [
@@ -127,19 +128,19 @@
     def iota(shape, axis):
         return lax.broadcasted_iota(jnp.int32, shape, axis)
 
-    def shift_rows(block, target, first, count):
+    def shift_rows(block, target, first, count, lows):
         lane = iota(block.shape, 1)
-        for low in range(LOWS):
+        for low in range(lows):
             piece = block
             if low:
                 piece = jnp.where(lane < block_len - low, pltpu.roll(block, block_len - low, 1), jnp.zeros_like(block))
             target[low * count + first:low * count + first + block.shape[0], :] = piece
 
-    def total_of(product, count, count_highs):
+    def total_of(product, count, count_highs, lows):
         lane = iota((count, 128), 1)
         sums = [product[0:count, 128 * i:128 * (i + 1)] for i in range(blocks)]
         for high in range(1, count_highs):
-            step = LOWS * high
+            step = lows * high
             turned = [
                 pltpu.roll(product[high * count:(high + 1) * count, 128 * i:128 * (i + 1)], 128 - step, 1)
                 for i in range(blocks)
@@ -166,7 +167,7 @@
             start = highs * first
             product = jnp.dot(select[band, start:start + highs * count, :], shifted[band],
                               preferred_element_type=f32)
-            sums = total_of(product, count, highs)
+            sums = total_of(product, count, highs, LOWS)
             for i in range(blocks):
                 outgoing[first // own_trials:(first + count) // own_trials, own_trials * band:own_trials * (band + 1),
                          128 * i:128 * (i + 1)] = sums[i].astype(bf16).reshape(count // own_trials, own_trials, 128)
@@ -190,7 +191,7 @@
     pick_trials(0, first_trials)
     loads[1].wait()
     for band in range(bands):
-        shift_rows(data_ref[band * CPS:(band + 1) * CPS, :], shifted.at[band], 0, CPS)
+        shift_rows(data_ref[band * CPS:(band + 1) * CPS, :], shifted.at[band], 0, CPS, LOWS)
     form(0, first_trials)
     last = me >= peers - 2
 
@@ -228,9 +229,9 @@
         delay = delay - (lane // half_rows).astype(f32)
         delay = jnp.where(lane % own_trials == iota((dms, 128), 0) // trial_dms, delay, -99.0)
         for high in range(sub_highs):
-            for pair in range(LOWS // 2):
+            for pair in range(SUB_LOWS // 2):
                 picks[half, high * dms:(high + 1) * dms, 128 * pair:128 * (pair + 1)] = jnp.where(
-                    delay == float(LOWS * high + 2 * pair), 1.0, 0.0).astype(bf16)
+                    delay == float(SUB_LOWS * high + 2 * pair), 1.0, 0.0).astype(bf16)
     before = jnp.where(iota((256, 256), 1) < 128, iota((256, 256), 0) % 128 - iota((256, 256), 1), -1) < 0
     totals[...] = before.astype(f32).astype(bf16)
 
@@ -240,12 +241,12 @@
         block = jnp.concatenate(
             [incoming[pl.ds(index * quarter, quarter), :, 128 * i:128 * (i + 1)].reshape(rows // 4, 128)
              for i in range(blocks)], axis=1)
-        shift_rows(block, moved.at[index // 2], place * (rows // 4), half_rows)
+        shift_rows(block, moved.at[index // 2], place * (rows // 4), half_rows, SUB_LOWS)
 
     def half_series(half):
         arrived(2 * half, 0)
         arrived(2 * half + 1, 1)
-        return total_of(jnp.dot(picks[half], moved[half], preferred_element_type=f32), dms, sub_highs)
+        return total_of(jnp.dot(picks[half], moved[half], preferred_element_type=f32), dms, sub_highs, SUB_LOWS)
 
     near = (2 * me) // peers
     series = [a + b for a, b in zip(half_series(near), half_series(1 - near))]
@@ -297,7 +298,7 @@
     dms = sub_delay.shape[0]
     group = bands * (NSDM // peers)
     highs = D1MAX // LOWS + 1
-    sub_highs = D2MAX // LOWS + 1
+    sub_highs = D2MAX // SUB_LOWS + 1
     anywhere = pl.BlockSpec(memory_space=pl.ANY)
     peaks = pl.pallas_call(
         functools.partial(fused_kernel, peers, block_len),
@@ -312,8 +313,8 @@
             pltpu.SemaphoreType.DMA((4,)),
             pltpu.VMEM((bands, highs * NSDM, LOWS * CPS), jnp.bfloat16),
             pltpu.VMEM((bands, LOWS * CPS, block_len), jnp.bfloat16),
-            pltpu.VMEM((2, sub_highs * dms, LOWS * rows // 2), jnp.bfloat16),
-            pltpu.VMEM((2, LOWS * rows // 2, block_len), jnp.bfloat16),
+            pltpu.VMEM((2, sub_highs * dms, SUB_LOWS * rows // 2), jnp.bfloat16),
+            pltpu.VMEM((2, SUB_LOWS * rows // 2, block_len), jnp.bfloat16),
             pltpu.VMEM((peers, group, block_len), jnp.bfloat16),
             pltpu.VMEM((peers, group, block_len), jnp.bfloat16),
             pltpu.VMEM((block_len, 2 * dms), jnp.float32),

time: 12.8 us -> 12.7 us (level)
  no operation moved by 1% of the time
where the time goes in v5:
time: 12.7 us; the launch traced here: 12.6 us
  Pallas kernels  12 us (94%)
  local copies, waits for them, and re-layouts  0.6 us (5%)
    pallas_call x1, Pallas kernels, fused(): pl.pallas_call(functools.partial(fused_kernel, peers, block_len), out_sha...  12 us
    unnamed x1, local copies, waits for them, and re-layouts  0.6 us

profile of v5, /device:TPU:0, one launch (start us, length us, event | category | flops | bytes accessed | tf_op | source)
XLA Modules:
  0.0 12.6 jit_solution(18318160636158743571)
XLA Ops:
  0.0 12.0 %shard_map.46 = f32[16,64]{1,0:T(8,128)S(1)} custom-call(bf16[128,640]{1,0:T(8,128)(2,1)} %data_hbm.1, s32[64,128]{1,0:T(8,128)} %chan_hbm.1, s32[64,64]{1,0:T(8,128)} %sub_hbm.1, s32[16]{0:T(128)} %width_hbm.1), custom_call_target="tpu_custom_call" | custom-call | tf_op jit(solution)/shard_map/pallas_call | solution.py:303
  12.0 0.6 %copy.6 = f32[64,16]{0,1:T(8,128)} copy(f32[64,16]{0,1:T(8,128)S(1)} %bitcast.1) | data formatting | bytes 8192

commit v6 on v5

--- a/solution.py
+++ b/solution.py
@@ -235,18 +235,18 @@
     before = jnp.where(iota((256, 256), 1) < 128, iota((256, 256), 0) % 128 - iota((256, 256), 1), -1) < 0
     totals[...] = before.astype(f32).astype(bf16)
 
-    def arrived(index, place):
-        part = incoming.at[pl.ds(index * quarter, quarter)]
-        pltpu.make_async_copy(part, part, recv_sem.at[index]).wait()
+    def half_series(half):
+        for index in (2 * half, 2 * half + 1):
+            part = incoming.at[pl.ds(index * quarter, quarter)]
+            pltpu.make_async_copy(part, part, recv_sem.at[index]).wait()
         block = jnp.concatenate(
-            [incoming[pl.ds(index * quarter, quarter), :, 128 * i:128 * (i + 1)].reshape(rows // 4, 128)
+            [incoming[pl.ds(2 * half * quarter, 2 * quarter), :, 128 * i:128 * (i + 1)].reshape(half_rows, 128)
              for i in range(blocks)], axis=1)
-        shift_rows(block, moved.at[index // 2], place * (rows // 4), half_rows, SUB_LOWS)
-
-    def half_series(half):
-        arrived(2 * half, 0)
-        arrived(2 * half + 1, 1)
-        return total_of(jnp.dot(picks[half], moved[half], preferred_element_type=f32), dms, sub_highs, SUB_LOWS)
+        padded = jnp.concatenate([block, jnp.zeros((half_rows, 128), bf16)], axis=1)
+        pieces = [block] + [
+            pltpu.roll(padded, block_len + 128 - low, 1)[:, 0:block_len] for low in range(1, SUB_LOWS)]
+        product = jnp.dot(picks[half], jnp.concatenate(pieces, axis=0), preferred_element_type=f32)
+        return total_of(product, dms, sub_highs, SUB_LOWS)
 
     near = (2 * me) // peers
     series = [a + b for a, b in zip(half_series(near), half_series(1 - near))]
@@ -281,8 +281,11 @@
             rise = running[pl.ds(widths[index] + start, tile), :] - base
             rise = jnp.max(rise.reshape(tile // 8, 8, 2 * dms), axis=0)
             best[index] = rise if start == 0 else jnp.maximum(best[index], rise)
-    peaks = [jnp.max(rise, axis=0, keepdims=True) for rise in best]
-    peaks = jnp.concatenate(peaks, axis=0)
+    for index in range(count):
+        running[8 * index:8 * index + 8, :] = best[index]
+    peaks = running[pl.ds(0, count, stride=8), :]
+    for within in range(1, 8):
+        peaks = jnp.maximum(peaks, running[pl.ds(within, count, stride=8), :])
     peaks = jnp.maximum(peaks, pltpu.roll(peaks, dms, 1))
     scales = jnp.concatenate(
         [jnp.full((1, dms), width_ref[index].astype(f32)) for index in range(width_ref.shape[0])], axis=0)

time: 12.7 us -> 12.6 us (level)
  Pallas kernels: 12 us -> 11.8 us
    pallas_call x1, Pallas kernels: 12 us -> 11.8 us  [fused(): pl.pallas_call(functools.partial(fused_kernel, peers, block_len), out_sha...]
where the time goes in v6:
time: 12.6 us; the launch traced here: 12.4 us
  Pallas kernels  11.8 us (94%)
  local copies, waits for them, and re-layouts  0.6 us (5%)
    pallas_call x1, Pallas kernels, fused(): pl.pallas_call(functools.partial(fused_kernel, peers, block_len), out_sha...  11.8 us
    unnamed x1, local copies, waits for them, and re-layouts  0.6 us

profile of v6, /device:TPU:0, one launch (start us, length us, event | category | flops | bytes accessed | tf_op | source)
XLA Modules:
  0.0 12.4 jit_solution(10116126737398919031)
XLA Ops:
  0.0 11.8 %shard_map.46 = f32[16,64]{1,0:T(8,128)S(1)} custom-call(bf16[128,640]{1,0:T(8,128)(2,1)} %data_hbm.1, s32[64,128]{1,0:T(8,128)} %chan_hbm.1, s32[64,64]{1,0:T(8,128)} %sub_hbm.1, s32[16]{0:T(128)} %width_hbm.1), custom_call_target="tpu_custom_call" | custom-call | tf_op jit(solution)/shard_map/pallas_call | solution.py:306
  11.8 0.6 %copy.6 = f32[64,16]{0,1:T(8,128)} copy(f32[64,16]{0,1:T(8,128)S(1)} %bitcast.1) | data formatting | bytes 8192

commit v7 on v6

--- a/solution.py
+++ b/solution.py
@@ -90,12 +90,12 @@
     local_peaks = peak_scores(normed, widths, block_len)
     return lax.pmax(local_peaks, "tm")
 
-LOWS = 4
+LOWS = 8
 SUB_LOWS = 8
 
 
 def fused_kernel(peers, block_len, data_hbm, chan_hbm, sub_hbm, width_hbm, out_ref,
-                 data_ref, chan_ref, sub_ref, width_ref, load_sem, select, shifted, picks, moved, outgoing, incoming,
+                 data_ref, chan_ref, sub_ref, width_ref, load_sem, select, shifted, picks, outgoing, incoming,
                  running, totals, send_sem, recv_sem):
     me = lax.axis_index("freq")
     rows = data_ref.shape[0]
@@ -129,11 +129,9 @@
         return lax.broadcasted_iota(jnp.int32, shape, axis)
 
     def shift_rows(block, target, first, count, lows):
-        lane = iota(block.shape, 1)
+        padded = jnp.concatenate([block, jnp.zeros((block.shape[0], 128), block.dtype)], axis=1)
         for low in range(lows):
-            piece = block
-            if low:
-                piece = jnp.where(lane < block_len - low, pltpu.roll(block, block_len - low, 1), jnp.zeros_like(block))
+            piece = pltpu.roll(padded, block_len + 128 - low, 1)[:, 0:block_len] if low else block
             target[low * count + first:low * count + first + block.shape[0], :] = piece
 
     def total_of(product, count, count_highs, lows):
@@ -317,7 +315,6 @@
             pltpu.VMEM((bands, highs * NSDM, LOWS * CPS), jnp.bfloat16),
             pltpu.VMEM((bands, LOWS * CPS, block_len), jnp.bfloat16),
             pltpu.VMEM((2, sub_highs * dms, SUB_LOWS * rows // 2), jnp.bfloat16),
-            pltpu.VMEM((2, SUB_LOWS * rows // 2, block_len), jnp.bfloat16),
             pltpu.VMEM((peers, group, block_len), jnp.bfloat16),
             pltpu.VMEM((peers, group, block_len), jnp.bfloat16),
             pltpu.VMEM((block_len, 2 * dms), jnp.float32),

time: 12.6 us -> 12.6 us (level)
  no operation moved by 1% of the time
where the time goes in v7:
time: 12.6 us; the launch traced here: 12.4 us
  Pallas kernels  11.8 us (94%)
  local copies, waits for them, and re-layouts  0.6 us (5%)
    pallas_call x1, Pallas kernels, fused(): pl.pallas_call(functools.partial(fused_kernel, peers, block_len), out_sha...  11.8 us
    unnamed x1, local copies, waits for them, and re-layouts  0.6 us

profile of v7, /device:TPU:0, one launch (start us, length us, event | category | flops | bytes accessed | tf_op | source)
XLA Modules:
  0.0 12.4 jit_solution(2566797411361306134)
XLA Ops:
  0.0 11.8 %shard_map.46 = f32[16,64]{1,0:T(8,128)S(1)} custom-call(bf16[128,640]{1,0:T(8,128)(2,1)} %data_hbm.1, s32[64,128]{1,0:T(8,128)} %chan_hbm.1, s32[64,64]{1,0:T(8,128)} %sub_hbm.1, s32[16]{0:T(128)} %width_hbm.1), custom_call_target="tpu_custom_call" | custom-call | tf_op jit(solution)/shard_map/pallas_call | solution.py:304
  11.8 0.6 %copy.6 = f32[64,16]{0,1:T(8,128)} copy(f32[64,16]{0,1:T(8,128)S(1)} %bitcast.1) | data formatting | bytes 8192
